TPU v7x, 32 devices: a whole 2x2x4 slice. The times are simulated.
32 devices in a mesh: clip: 2 (over y), height: 4 (over z), head: 4 (over x, core).
Axes of the slice: x: 2, y: 2, z: 4, core: 2. Of those that a mesh axis runs over, the one named last changes fastest.
Arguments:
- tokens: bfloat16 [8, 192, 5120], P(('clip', 'height'), None, 'head'), parts along dimension 0, may hold values from -6 to 6
- in_sign: int32 [5120], replicated, may hold values from 0 to 1
- qkv_codes: int32 [640, 3, 3072], P(None, None, 'head'), may hold values from 0 to 65535
- qkv_scale: float32 [3, 3072], P(None, 'head'), may hold values from 0.3 to 3
- qkv_sign: int32 [3, 3072], P(None, 'head'), may hold values from 0 to 1
- windows: int32 [8, 3, 27], P(('clip', 'height')), parts along dimension 0, may hold values from 0 to 11, as said below
- oin_sign: int32 [3072], P('head'), may hold values from 0 to 1
- out_codes: int32 [384, 5120], P('head'), may hold values from 0 to 65535
- out_scale: float32 [5120], replicated, may hold values from 2 to 20
- out_sign: int32 [5120], replicated, may hold values from 0 to 1
Outputs:
- attention_out: bfloat16 [8, 192, 5120], P(('clip', 'height'), 'head'), parts along dimension 0
There are 2 independent parts, one for each index of `clip`. A program takes and returns all parts, laid end to end along the dimension named above; an argument that names none is the same for every part. Nothing has to cross between parts.
Inputs may be any that keep to these rules, and one draw needn't show every extreme that they name: `windows`: each row lists the query tile itself and 26 further entries, each one of the 27 tiles of the 3 x 3 x 3 block of tiles centred on the query tile (each of the three coordinates clipped into the grid of 1 x 4 x 3 tiles); entries may repeat and appear in any order.
All inputs are finite; a program needn't handle non-finite values.
Results may differ from a plain program's by a relative error of at most 0.015.
Values may be sent and summed in bfloat16 or wider, within the bound.
A program may use at most 128 MiB of HBM per device.

v0:
```python
import functools

import jax
import jax.numpy as jnp
import numpy as np
from jax import lax
from jax.experimental import pallas as pl
from jax.experimental.pallas import tpu as pltpu
from jax.sharding import PartitionSpec as P

HD = 128
HAD = 128
TILE = 64
HROWS = 4
PLANES = 8
GROUP = HAD // PLANES
EPSILON = 1e-06
MESH = pl.DeviceIdType.MESH
VLIMIT = 60 * 1024 * 1024


def sylvester(order_size):
    matrix_now = np.ones((1, 1), np.float32)
    seed_pair = np.array([[1.0, 1.0], [1.0, -1.0]], np.float32)
    while matrix_now.shape[0] < order_size:
        matrix_now = np.kron(matrix_now, seed_pair)
    return matrix_now


ORDER = np.array([8 * i + k for k in range(PLANES) for i in range(GROUP)])
PLANE_POWER = np.array([4.0**k for k in range(PLANES) for _ in range(GROUP)], np.float32)


def plain_matrix():
    return jnp.asarray(sylvester(HAD), jnp.bfloat16)


def plane_matrix():
    return jnp.asarray(sylvester(HAD)[:, ORDER], jnp.bfloat16)


def plane_scale():
    return jnp.asarray((HAD**-0.5 / PLANE_POWER)[None, :], jnp.float32)


def plane_power():
    return jnp.asarray(PLANE_POWER[None, :], jnp.float32)


def signed(sign_bits):
    return (2 * sign_bits - 1).astype(jnp.float32)


def dot(left, right):
    return jnp.dot(left, right, preferred_element_type=jnp.float32)


def rotate_split(block, matrix):
    high = block.astype(jnp.bfloat16)
    low = (block - high.astype(jnp.float32)).astype(jnp.bfloat16)
    return (dot(high, matrix) + dot(low, matrix)) * HAD**-0.5


def unpack_block(words):
    planes = [(words & (3 << (2 * k))).astype(jnp.float32).astype(jnp.bfloat16) for k in range(PLANES)]
    pieces = []
    for block in range(words.shape[0] // GROUP):
        for k in range(PLANES):
            pieces.append(planes[k][block * GROUP : (block + 1) * GROUP])
    return jnp.concatenate(pieces, axis=0)


def row_sums(rows, power):
    total = None
    for block in range(rows.shape[1] // HAD):
        part = rows[:, block * HAD : (block + 1) * HAD].astype(jnp.float32) * power
        total = part if total is None else total + part
    return jnp.sum(total, axis=1, keepdims=True)


def layer_kernel(
    n, peers, distances, cols, gcols,
    x_ref, insigns_ref, qscale_ref, qsign_ref, listed_ref, osign_ref, oscale_ref, outsign_ref,
    plane_mat_ref, mat_ref, pscale_ref, power_ref, codes_ref, ocodes_ref,
    out_ref,
    turned, words, weights, acc, offset, qkv, near, owords, oweights, gathered, totals,
    rotated, ooffset, lines, insigns, part, word_sem, oword_sem, halo_send, halo_recv, *scratch,
):
    me = lax.axis_index("head")
    row = lax.axis_index("height")
    rows, width = x_ref.shape
    count = words.shape[0]
    per_part = count // 3
    per_chunk = cols // HD
    local = per_part * cols
    depth = width // PLANES
    qtiles = rows // TILE
    groups = part.shape[0]
    share = rows // n
    slots = len(distances)

    def fetch(j):
        return pltpu.make_async_copy(
            codes_ref.at[(j // per_part + 1) % 3, :, pl.ds(pl.multiple_of(j % per_part * cols, HD), cols)],
            words.at[j],
            word_sem.at[j],
        )

    for j in range(count):
        fetch(j).start()
    fetch_out = pltpu.make_async_copy(ocodes_ref, owords, oword_sem)
    fetch_out.start()

    barrier = pltpu.get_barrier_semaphore()
    if n == 4:
        partner = me + 1 - 2 * (me % 2)
        across = (me + 2) % 4
        diagonal = (partner + 2) % 4
        head_peers = [partner, across]
        early, late = [me, partner], [across, diagonal]
    else:
        head_peers = [(me + p) % n for p in range(1, n)]
        early, late = [me], head_peers
    gives = [jnp.logical_and(row + d >= 0, row + d < peers) for d in distances]
    takes = [jnp.logical_and(row - d >= 0, row - d < peers) for d in distances]
    for peer in head_peers:
        pl.semaphore_signal(barrier, inc=1, device_id={"head": peer}, device_id_type=MESH)
    greeted = jnp.int32(len(head_peers))
    for slot, distance in enumerate(distances):

        @pl.when(gives[slot])
        def _():
            pl.semaphore_signal(
                barrier, inc=1, device_id={"height": row + distance}, device_id_type=MESH
            )

        greeted = greeted + jnp.where(gives[slot], 1, 0)

    for shard in range(n):
        for block in range(width // HAD):
            lanes = slice(block * HAD, (block + 1) * HAD)
            line = signed(insigns_ref[shard * width + block * HAD : shard * width + (block + 1) * HAD])
            insigns[shard, :, lanes] = jnp.broadcast_to(line[None, :], (8, HAD))
    for block in range(width // HAD):
        lanes = slice(block * HAD, (block + 1) * HAD)
        spun = dot(x_ref[:, lanes] * insigns[me, 0:1, lanes].astype(jnp.bfloat16), plane_mat_ref[...])
        turned[me, :, lanes] = (spun * pscale_ref[...]).astype(jnp.bfloat16)
    for j in range(count):
        source = (j // per_part + 1) % 3
        spots = slice(j % per_part * cols, (j % per_part + 1) * cols)
        scale = qscale_ref[source : source + 1, spots] * (width * n) ** -0.5
        sign = signed(qsign_ref[source : source + 1, spots])
        lines[j, 0:8, :] = jnp.broadcast_to(scale, (8, cols))
        lines[j, 8:16, :] = jnp.broadcast_to(sign, (8, cols))
    pl.semaphore_wait(barrier, greeted)

    def head_copy(src, dst, send, recv, peer):
        return pltpu.make_async_remote_copy(
            src, dst, send, recv, device_id={"head": peer}, device_id_type=MESH
        )

    def unpack(j):
        fetch(j).wait()
        for shard in range(n):
            weights[j, shard] = unpack_block(words[j, shard * depth : (shard + 1) * depth, :])
        total = dot(turned[early[0]], weights[j, early[0]])
        for shard in early[1:]:
            total = total + dot(turned[shard], weights[j, shard])
        acc[j] = total

    if n == 4:
        a_send, a_recv, f_send, f_recv, b_send, b_recv = scratch[:6]
        scratch = scratch[6:]
        chunks = a_send.shape[0]
        step = rows // chunks

        def piece(slot, c):
            return turned.at[slot, pl.ds(c * step, step), :]

        crossing = [
            head_copy(piece(me, c), piece(me, c), a_send.at[c], a_recv.at[c], across)
            for c in range(chunks)
        ]
        relays = [
            head_copy(piece(across, c), piece(across, c), f_send.at[c], f_recv.at[c], partner)
            for c in range(chunks)
        ]
        for copy in crossing:
            copy.start()
        beside = head_copy(turned.at[me], turned.at[me], b_send, b_recv, partner)
        beside.start()
        beside.wait_recv()
        done = 0
        for c in range(chunks):
            upto = count * (c + 1) // chunks

            @pl.loop(done, upto)
            def _(j):
                unpack(j)

            done = upto
            crossing[c].wait_recv()
            relays[c].start()
        for copy in relays:
            copy.wait_recv()
        sent = crossing + relays + [beside]
    else:
        g_send, g_recv = scratch[:2]
        scratch = scratch[2:]
        sent = [
            head_copy(turned.at[me], turned.at[me], g_send.at[p], g_recv.at[p], peer)
            for p, peer in enumerate(head_peers)
        ]
        for copy in sent:
            copy.start()

        @pl.loop(0, count)
        def _(j):
            unpack(j)

        for copy in sent:
            copy.wait_recv()

    total = jnp.zeros((rows, 1), jnp.float32)
    for shard in range(n):
        total = total + row_sums(turned[shard], power_ref[...])
    offset[...] = jnp.broadcast_to(1.5 * total, offset.shape)

    def finish(j):
        result = acc[j]
        for shard in late:
            result = result + dot(turned[shard], weights[j, shard])
        source = (j // per_part + 1) % 3
        for head in range(per_chunk):
            lanes = slice(head * HD, (head + 1) * HD)
            block = (result[:, lanes] - offset[...]) * lines[j, 0:1, lanes]
            block = rotate_split(block, mat_ref[...]) * lines[j, 8:9, lanes]
            mean = jnp.mean(block * block, axis=-1, keepdims=True)
            divisor = jnp.where(source < 2, jnp.sqrt(mean + EPSILON), 1.0)
            qkv[j, :, lanes] = (block / divisor).astype(jnp.bfloat16)

    def halo_copy(slot, j):
        return pltpu.make_async_remote_copy(
            qkv.at[j], near.at[slot, j], halo_send.at[slot, j], halo_recv.at[slot, j],
            device_id={"height": row + distances[slot]}, device_id_type=MESH,
        )

    @pl.loop(0, 2 * per_part)
    def _(j):
        finish(j)
        for slot in range(slots):

            @pl.when(gives[slot])
            def _():
                halo_copy(slot, j).start()

    for slot in range(slots):

        @pl.when(jnp.logical_not(takes[slot]))
        def _():
            near[slot] = jnp.zeros(near.shape[1:], near.dtype)

    @pl.loop(2 * per_part, count)
    def _(j):
        finish(j)

    def mask_of(first_tile):
        ids = lax.broadcasted_iota(jnp.int32, (8, rows), 1) // TILE + first_tile
        stack = []
        for tile in range(qtiles):
            hit = ids == listed_ref[tile, 0, 0]
            for entry in range(1, listed_ref.shape[2]):
                hit = jnp.logical_or(hit, ids == listed_ref[tile, 0, entry])
            stack.extend([jnp.where(hit, 1.0, 0.0)] * (TILE // 8))
        return jnp.concatenate(stack, axis=0)

    def attend(queries, keys, values, mask):
        score = lax.dot_general(
            queries, keys, (((1,), (1,)), ((), ())), preferred_element_type=jnp.float32
        )
        weight = jnp.exp(score * HD**-0.5) * mask
        return dot(weight.astype(jnp.bfloat16), values), jnp.sum(weight, axis=-1, keepdims=True)

    own_mask = mask_of(row * qtiles)
    near_masks = [mask_of((row - d) * qtiles) for d in distances]
    for head in range(local // HD):
        chunk, lanes = head // per_chunk, slice(head % per_chunk * HD, (head % per_chunk + 1) * HD)
        found, sums = attend(
            qkv[2 * per_part + chunk, :, lanes], qkv[chunk, :, lanes],
            qkv[per_part + chunk, :, lanes], own_mask,
        )
        gathered[head] = found
        totals[head] = jnp.broadcast_to(sums, found.shape)

    fetch_out.wait()

    @pl.loop(0, groups)
    def _(g):
        spots = pl.ds(pl.multiple_of(g * gcols, HD), gcols)
        oweights[g] = unpack_block(owords[:, spots])

    for head in range(local // HD):
        chunk, lanes = head // per_chunk, slice(head % per_chunk * HD, (head % per_chunk + 1) * HD)
        if head % per_chunk == 0:
            for slot in range(slots):

                @pl.when(takes[slot])
                def _():
                    halo_copy(slot, chunk).wait_recv()
                    halo_copy(slot, per_part + chunk).wait_recv()

        found, sums = gathered[head], totals[head]
        for slot in range(slots):
            more, more_sums = attend(
                qkv[2 * per_part + chunk, :, lanes], near[slot, chunk, :, lanes],
                near[slot, per_part + chunk, :, lanes], near_masks[slot],
            )
            found, sums = found + more, sums + more_sums
        attended = (found / sums).astype(jnp.bfloat16)
        spots = slice(head * HD, (head + 1) * HD)
        spun = dot(attended * signed(osign_ref[spots])[None, :].astype(jnp.bfloat16), plane_mat_ref[...])
        rotated[:, spots] = (spun * pscale_ref[...]).astype(jnp.bfloat16)
    ooffset[...] = jnp.broadcast_to(1.5 * row_sums(rotated[...], power_ref[...]), ooffset.shape)

    def produce(g):
        result = dot(rotated[...], oweights[g])
        for block in range(gcols // HAD):
            lanes = slice(block * HAD, (block + 1) * HAD)
            spots = slice(g * gcols + block * HAD, g * gcols + (block + 1) * HAD)
            value = (result[:, lanes] - ooffset[...]) * (oscale_ref[spots] * (local * n) ** -0.5)[None, :]
            part[g, :, :, lanes] = value.reshape(n, share, HAD).astype(jnp.bfloat16)

    def conclude(g, terms):
        for block in range(gcols // HAD):
            lanes = slice(block * HAD, (block + 1) * HAD)
            spots = slice(g * gcols + block * HAD, g * gcols + (block + 1) * HAD)
            total = part[g, me, :, lanes].astype(jnp.float32)
            for term in terms:
                total = total + term[:, lanes].astype(jnp.float32)
            spun = rotate_split(total, mat_ref[...]) * signed(outsign_ref[spots])[None, :]
            out_ref[:, spots] = spun.astype(jnp.bfloat16)

    if n == 4:
        staged, flank, summed, crossed, p_send, p_recv, q_send, q_recv, x_send, x_recv = scratch
        first = [
            head_copy(part.at[g, diagonal], staged.at[g], p_send.at[g], p_recv.at[g], partner)
            for g in range(groups)
        ]
        second = [
            head_copy(part.at[g, partner], flank.at[g], q_send.at[g], q_recv.at[g], partner)
            for g in range(groups)
        ]
        third = [
            head_copy(summed.at[g], crossed.at[g], x_send.at[g], x_recv.at[g], across)
            for g in range(groups)
        ]

        def relay(g):
            first[g].wait_recv()
            summed[g] = (
                part[g, across].astype(jnp.float32) + staged[g].astype(jnp.float32)
            ).astype(jnp.bfloat16)
            third[g].start()

        for g in range(groups):
            produce(g)
            first[g].start()
            second[g].start()
            if g > 0:
                relay(g - 1)
        relay(groups - 1)
        for g in range(groups):
            second[g].wait_recv()
            third[g].wait_recv()
            conclude(g, [flank[g], crossed[g]])
        sent = sent + first + second + third
    else:
        landed, r_send, r_recv = scratch
        moves = []
        for g in range(groups):
            produce(g)
            move = [
                head_copy(part.at[g, peer], landed.at[p, g], r_send.at[p, g], r_recv.at[p, g], peer)
                for p, peer in enumerate(head_peers)
            ]
            for copy in move:
                copy.start()
            moves.append(move)
        for g in range(groups):
            for copy in moves[g]:
                copy.wait_recv()
            conclude(g, [landed[p, g] for p in range(n - 1)])
        sent = sent + [copy for move in moves for copy in move]

    for copy in sent:
        copy.wait_send()
    for slot in range(slots):

        @pl.when(gives[slot])
        def _():
            for j in range(2 * per_part):
                halo_copy(slot, j).wait_send()


def on_device(
    n,
    peers,
    tokens,
    in_sign,
    qkv_codes,
    qkv_scale,
    qkv_sign,
    windows,
    oin_sign,
    out_codes,
    out_scale,
    out_sign,
):
    own = tokens[0]
    rows, width = own.shape
    local = qkv_scale.shape[1]
    features = out_codes.shape[1]
    reach = (1,) if peers <= HROWS else (1, HROWS - 1, HROWS, HROWS + 1)
    distances = tuple(d for r in reach if r < peers for d in (r, -r))
    slots = len(distances)
    cols = 256 if local % 256 == 0 else HD
    count = 3 * local // cols
    per_part = count // 3
    inner = qkv_codes.shape[0]
    gcols = 1024 if features % 1024 == 0 else HD
    groups = features // gcols
    share = rows // n
    chunks = 4
    dma = pltpu.SemaphoreType.DMA
    grouped = pltpu.VMEM((groups, share, gcols), jnp.bfloat16)
    if n == 4:
        tail = [dma((chunks,))] * 4 + [dma] * 2 + [grouped] * 4 + [dma((groups,))] * 6
    else:
        tail = [dma((n - 1,))] * 2
        tail += [pltpu.VMEM((n - 1, groups, share, gcols), jnp.bfloat16)]
        tail += [dma((n - 1, groups))] * 2
    vmem = pl.BlockSpec(memory_space=pltpu.VMEM)
    anywhere = pl.BlockSpec(memory_space=pl.ANY)
    smem = pl.BlockSpec(memory_space=pltpu.SMEM)
    result = pl.pallas_call(
        functools.partial(layer_kernel, n, peers, distances, cols, gcols),
        name="layer",
        out_shape=jax.ShapeDtypeStruct((share, features), jnp.bfloat16),
        in_specs=[vmem] * 4 + [smem] + [vmem] * 7 + [anywhere] * 2,
        out_specs=vmem,
        scratch_shapes=[
            pltpu.VMEM((n, rows, width), jnp.bfloat16),
            pltpu.VMEM((count, inner, cols), jnp.int32),
            pltpu.VMEM((count, n, width, cols), jnp.bfloat16),
            pltpu.VMEM((count, rows, cols), jnp.float32),
            pltpu.VMEM((rows, HD), jnp.float32),
            pltpu.VMEM((count, rows, cols), jnp.bfloat16),
            pltpu.VMEM((slots, 2 * per_part, rows, cols), jnp.bfloat16),
            pltpu.VMEM(out_codes.shape, jnp.int32),
            pltpu.VMEM((groups, local, gcols), jnp.bfloat16),
            pltpu.VMEM((local // HD, rows, HD), jnp.float32),
            pltpu.VMEM((local // HD, rows, HD), jnp.float32),
            pltpu.VMEM((rows, local), jnp.bfloat16),
            pltpu.VMEM((rows, HD), jnp.float32),
            pltpu.VMEM((count, 16, cols), jnp.float32),
            pltpu.VMEM((n, 8, width), jnp.float32),
            pltpu.VMEM((groups, n, share, gcols), jnp.bfloat16),
            dma((count,)),
            dma,
            dma((slots, 2 * per_part)),
            dma((slots, 2 * per_part)),
        ]
        + tail,
        compiler_params=pltpu.CompilerParams(
            collective_id=0, has_side_effects=True, vmem_limit_bytes=VLIMIT
        ),
    )(
        own,
        in_sign,
        qkv_scale,
        qkv_sign,
        jnp.transpose(windows, (1, 0, 2)),
        oin_sign,
        out_scale,
        out_sign,
        plane_matrix(),
        plain_matrix(),
        plane_scale(),
        plane_power(),
        jnp.transpose(qkv_codes, (1, 0, 2)),
        out_codes,
    )
    return result[None]


def solution(mesh):
    n = mesh.shape["head"]
    peers = mesh.shape["height"]
    return jax.shard_map(
        functools.partial(on_device, n, peers),
        mesh=mesh,
        in_specs=(
            P(("clip", "height"), None, "head"),
            P(),
            P(None, None, "head"),
            P(None, "head"),
            P(None, "head"),
            P(("clip", "height"), None, None),
            P("head"),
            P("head", None),
            P(),
            P(),
        ),
        out_specs=P(("clip", "height"), "head", None),
        check_vma=False,
    )
```

profile of v0, /device:TPU:0, one launch (start us, length us, event | category | flops | bytes accessed | tf_op | source)
XLA Modules:
  0.0 52.8 jit_solution(8551836788947365502)
XLA Ops:
  0.0 50.9 %layer.1 = bf16[48,5120]{1,0:T(8,128)(2,1)} custom-call(bf16[192,1280]{1,0:T(8,128)(2,1)} %bitcast.6, s32[5120]{0:T(1024)} %insigns_ref.1, f32[3,768]{1,0:T(4,128)} %qscale_ref.1, s32[3,768]{1,0:T(4,128)} %qsign_ref.1, s32[3,1,27]{2,1,0:T(1,128)} %bitcast.7, s32[768]{0:T(1024)} %osign_ref.1, f32[5120]{0:T(1024)} %oscale_ref.1, s32[5120]{0:T(1024)} %outsign_ref.1, ...), custom_call_target="tpu_custom_call" | custom-call | tf_op jit(solution)/shard_map/layer/pallas_call | solution.py:445
  50.9 1.8 %copy.16 = bf16[1,48,5120]{2,1,0:T(8,128)(2,1)} copy(bf16[1,48,5120]{2,1,0:T(8,128)(2,1)} %bitcast.5) | data formatting | bytes 983040
where the time goes:
time: 52.9 us; the launch traced here: 52.8 us
  Pallas kernels  50.9 us (96%)
  local copies, waits for them, and re-layouts  1.84 us (3%)
    pallas_call x1, Pallas kernels, on_device(): pl.pallas_call(functools.partial(layer_kernel, n, peers, distances, cols,...  50.9 us
    unnamed x1, local copies, waits for them, and re-layouts  1.84 us

commit v1 on v0

--- a/solution.py
+++ b/solution.py
@@ -45,6 +45,10 @@
 
 def plane_power():
     return jnp.asarray(PLANE_POWER[None, :], jnp.float32)
+
+
+def power_matrix():
+    return jnp.asarray(np.repeat(PLANE_POWER[:, None], HAD, axis=1), jnp.bfloat16)
 
 
 def signed(sign_bits):
@@ -402,6 +406,502 @@
                 halo_copy(slot, j).wait_send()
 
 
+def quad_kernel(
+    peers,
+    x_ref, insigns_ref, qscale_ref, qsign_ref, listed_ref, osign_ref, oscale_ref, outsign_ref,
+    plane_mat_ref, mat_ref, pscale_ref, pmat_ref, codes_ref, ocodes_ref,
+    out_ref,
+    early_x, late_x, words, early_w, late_w, acc, eoff, offs, pm, lines, insigns, kv, queries, near,
+    owords, oweights, num, tot, own_mask, near_mask, rotated, ooff, part, staged, summed, flank, crossed,
+    word_sem, oword_sem, a_send, a_recv, f_send, f_recv, b_send, b_recv, halo_send, halo_recv,
+    p_send, p_recv, r_send, r_recv, q_send, q_recv, x_send, x_recv,
+):
+    me = lax.axis_index("head")
+    row = lax.axis_index("height")
+    rows, width = x_ref.shape
+    count, _, cols = words.shape
+    per_part = count // 3
+    per_chunk = cols // HD
+    local = per_part * cols
+    depth = width // PLANES
+    groups, gcols = part.shape[0], part.shape[3]
+    steps = rows // TILE
+    unit = part.shape[2]
+    heads = local // HD
+    chip, core = me // 2, me % 2
+    partner = me + 1 - 2 * core
+    across = (me + 2) % 4
+    diagonal = (partner + 2) % 4
+    distances = (1, -1)
+
+    def tile_at(step):
+        return chip * step + (1 - chip) * (steps - 1 - step)
+
+    def fetch(j):
+        return pltpu.make_async_copy(
+            codes_ref.at[(j // per_part + 1) % 3, :, pl.ds(pl.multiple_of(j % per_part * cols, HD), cols)],
+            words.at[j],
+            word_sem.at[j],
+        )
+
+    for j in range(count):
+        fetch(j).start()
+    fetch_out = pltpu.make_async_copy(ocodes_ref, owords, oword_sem)
+    fetch_out.start()
+
+    barrier = pltpu.get_barrier_semaphore()
+    gives = [jnp.logical_and(row + d >= 0, row + d < peers) for d in distances]
+    takes = [jnp.logical_and(row - d >= 0, row - d < peers) for d in distances]
+    for peer in (partner, across, diagonal):
+        pl.semaphore_signal(barrier, inc=1, device_id={"head": peer}, device_id_type=MESH)
+    greeted = jnp.int32(3)
+    for slot, distance in enumerate(distances):
+
+        @pl.when(gives[slot])
+        def _():
+            pl.semaphore_signal(
+                barrier, inc=1, device_id={"height": row + distance}, device_id_type=MESH
+            )
+
+        greeted = greeted + jnp.where(gives[slot], 1, 0)
+
+    for shard in range(4):
+        for block in range(width // HAD):
+            lanes = slice(block * HAD, (block + 1) * HAD)
+            line = signed(insigns_ref[shard * width + block * HAD : shard * width + (block + 1) * HAD])
+            insigns[shard, :, lanes] = jnp.broadcast_to(line[None, :], (8, HAD))
+    for step in reversed(range(steps)):
+        start = pl.multiple_of(tile_at(step) * TILE, TILE)
+        for block in range(width // HAD):
+            lanes = slice(block * HAD, (block + 1) * HAD)
+            plain = x_ref[pl.ds(start, TILE), lanes] * insigns[me, 0:1, lanes].astype(jnp.bfloat16)
+            spun = dot(plain, plane_mat_ref[...])
+            early_x[0, step, :, lanes] = (spun * pscale_ref[...]).astype(jnp.bfloat16)
+
+    def head_copy(src, dst, send, recv, peer):
+        return pltpu.make_async_remote_copy(
+            src, dst, send, recv, device_id={"head": peer}, device_id_type=MESH
+        )
+
+    crossing = [
+        head_copy(early_x.at[0, steps - 1 - i], late_x.at[0, i], a_send.at[i], a_recv.at[i], across)
+        for i in range(steps)
+    ]
+    relays = [
+        head_copy(late_x.at[0, i], late_x.at[1, i], f_send.at[i], f_recv.at[i], partner)
+        for i in range(steps)
+    ]
+    beside = head_copy(early_x.at[0], early_x.at[1], b_send, b_recv, partner)
+    pl.semaphore_wait(barrier, greeted)
+    for copy in crossing:
+        copy.start()
+    beside.start()
+
+    for block in range(width // HAD):
+        pm[block * HAD : (block + 1) * HAD, :] = pmat_ref[...]
+    for j in range(count):
+        source = (j // per_part + 1) % 3
+        spots = slice(j % per_part * cols, (j % per_part + 1) * cols)
+        scale = qscale_ref[source : source + 1, spots] * (width * 4) ** -0.5
+        sign = signed(qsign_ref[source : source + 1, spots]) * HAD**-0.5
+        lines[j, 0:8, :] = jnp.broadcast_to(scale, (8, cols))
+        lines[j, 8:16, :] = jnp.broadcast_to(sign, (8, cols))
+    for slot in range(2):
+
+        @pl.when(jnp.logical_not(takes[slot]))
+        def _():
+            near[slot] = jnp.zeros(near.shape[1:], near.dtype)
+
+    def listed_mask(step, ids):
+        tile = tile_at(step)
+        hit = ids == listed_ref[tile, 0, 0]
+        for entry in range(1, listed_ref.shape[2]):
+            hit = jnp.logical_or(hit, ids == listed_ref[tile, 0, entry])
+        return jnp.where(hit, 1.0, 0.0)
+
+    own_ids = tile_at(lax.broadcasted_iota(jnp.int32, (8, rows), 1) // TILE) + row * steps
+    for step in range(steps):
+        own_mask[step] = listed_mask(step, own_ids)
+    side = lax.broadcasted_iota(jnp.int32, (8, 2 * TILE), 1) // TILE
+    side_row = row - 1 + 2 * side
+    for s in range(steps):
+        for step in range(steps):
+            if abs(s - step) < 2:
+                near_mask[s, step] = listed_mask(step, side_row * steps + tile_at(s))
+
+    shards = [me, partner, across, diagonal]
+
+    def unpack_role(j, role, target):
+        for block in range(depth // GROUP):
+            start = pl.multiple_of(shards[role] * depth + block * GROUP, GROUP)
+            block_words = words[j, pl.ds(start, GROUP), :]
+            for k in range(PLANES):
+                spot = block * HAD + k * GROUP
+                plane = (block_words & (3 << (2 * k))).astype(jnp.float32).astype(jnp.bfloat16)
+                target[role % 2, spot : spot + GROUP, :] = plane
+
+    def prepare(j):
+        fetch(j).wait()
+        for role in range(2):
+            unpack_role(j, role, early_w)
+        total = dot(early_x[0].reshape(rows, width), early_w[0])
+        total = total + dot(early_x[1].reshape(rows, width), early_w[1])
+        for role in range(2, 4):
+            unpack_role(j, role, late_w.at[j])
+        acc[j] = total.reshape(steps, TILE, cols)
+
+    beside.wait_recv()
+    total = dot(early_x[0].reshape(rows, width), pm[...])
+    total = total + dot(early_x[1].reshape(rows, width), pm[...])
+    eoff[...] = total.reshape(steps, TILE, HD)
+
+    def spread(c):
+        spots = pl.ds(pl.multiple_of(c * gcols, HD), gcols)
+        for block in range(owords.shape[0] // GROUP):
+            block_words = owords[block * GROUP : (block + 1) * GROUP, spots]
+            for k in range(PLANES):
+                spot = block * HAD + k * GROUP
+                plane = (block_words & (3 << (2 * k))).astype(jnp.float32).astype(jnp.bfloat16)
+                oweights[c, spot : spot + GROUP, :] = plane
+
+    def halo_copy(slot, step, c):
+        return pltpu.make_async_remote_copy(
+            kv.at[step, c], near.at[slot, step, c],
+            halo_send.at[slot, step, c], halo_recv.at[slot, step, c],
+            device_id={"height": row + distances[slot]}, device_id_type=MESH,
+        )
+
+    def project(step):
+        late = dot(late_x[0, step], pm[...]) + dot(late_x[1, step], pm[...])
+        offs[...] = 1.5 * (eoff[step] + late)
+
+        @pl.loop(0, per_part)
+        def _(c):
+            for kind in range(3):
+                j = kind * per_part + c
+                result = acc[j, step] + dot(late_x[0, step], late_w[j, 0])
+                result = result + dot(late_x[1, step], late_w[j, 1])
+                stack, factors = [], []
+                for head in range(per_chunk):
+                    lanes = slice(head * HD, (head + 1) * HD)
+                    block = (result[:, lanes] - offs[...]) * lines[j, 0:1, lanes]
+                    high = block.astype(jnp.bfloat16)
+                    stack += [high, (block - high.astype(jnp.float32)).astype(jnp.bfloat16)]
+                    if kind != 1:
+                        mean = jnp.mean(block * block, axis=-1, keepdims=True)
+                        factors.append(lax.rsqrt(mean + EPSILON))
+                spun = dot(jnp.concatenate(stack, axis=0), mat_ref[...])
+                for head in range(per_chunk):
+                    lanes = slice(head * HD, (head + 1) * HD)
+                    at = 2 * head * TILE
+                    value = (spun[at : at + TILE] + spun[at + TILE : at + 2 * TILE]) * lines[j, 8:9, lanes]
+                    if kind != 1:
+                        value = value * factors[head]
+                    if kind == 2:
+                        queries[step, c, :, lanes] = value.astype(jnp.bfloat16)
+                    else:
+                        kv[step, c, kind, :, lanes] = value.astype(jnp.bfloat16)
+            for slot in range(2):
+
+                @pl.when(gives[slot])
+                def _():
+                    halo_copy(slot, step, c).start()
+
+    @pl.loop(0, count - 2)
+    def _(j):
+        prepare(j)
+
+    crossing[0].wait_recv()
+    relays[0].start()
+
+    @pl.loop(count - 2, count)
+    def _(j):
+        prepare(j)
+
+    relays[0].wait_recv()
+    project(0)
+    crossing[1].wait_recv()
+    relays[1].start()
+    fetch_out.wait()
+
+    @pl.loop(0, 2)
+    def _(c):
+        spread(c)
+
+    relays[1].wait_recv()
+    project(1)
+    crossing[2].wait_recv()
+    relays[2].start()
+
+    @pl.loop(2, groups)
+    def _(c):
+        spread(c)
+
+    relays[2].wait_recv()
+    project(2)
+
+    def attend(rows_q, keys, values, mask):
+        score = lax.dot_general(
+            rows_q, keys, (((1,), (1,)), ((), ())), preferred_element_type=jnp.float32
+        )
+        weight = jnp.exp(score * HD**-0.5) * mask
+        return dot(weight.astype(jnp.bfloat16), values), jnp.sum(weight, axis=-1, keepdims=True)
+
+    def lanes_of(head):
+        return slice(head % per_chunk * HD, (head % per_chunk + 1) * HD)
+
+    def broad(masks):
+        return jnp.concatenate([jnp.broadcast_to(m[0:1], (TILE, m.shape[1])) for m in masks], axis=0)
+
+    everything = range(steps)
+    mask = broad([own_mask[a] for a in everything])
+    for head in range(heads):
+        c, lanes = head // per_chunk, lanes_of(head)
+        found, sums = attend(
+            jnp.concatenate([queries[a, c, :, lanes] for a in everything], axis=0),
+            jnp.concatenate([kv[a, c, 0, :, lanes] for a in everything], axis=0),
+            jnp.concatenate([kv[a, c, 1, :, lanes] for a in everything], axis=0),
+            mask,
+        )
+        num[:, head] = found.reshape(steps, TILE, HD)
+        tot[:, head] = jnp.broadcast_to(sums, found.shape).reshape(steps, TILE, HD)
+
+    def near_wait(s):
+        for slot in range(2):
+
+            @pl.when(takes[slot])
+            def _():
+                for c in range(per_part):
+                    halo_copy(slot, s, c).wait_recv()
+
+    def near_attend(s, over):
+        mask = broad([near_mask[s, a] for a in over])
+        for head in range(heads):
+            c, lanes = head // per_chunk, lanes_of(head)
+            found, sums = attend(
+                jnp.concatenate([queries[a, c, :, lanes] for a in over], axis=0),
+                jnp.concatenate([near[slot, s, c, 0, :, lanes] for slot in range(2)], axis=0),
+                jnp.concatenate([near[slot, s, c, 1, :, lanes] for slot in range(2)], axis=0),
+                mask,
+            )
+            for at, a in enumerate(over):
+                span = slice(at * TILE, (at + 1) * TILE)
+                num[a, head] = num[a, head] + found[span]
+                tot[a, head] = tot[a, head] + sums[span]
+
+    def complete(over):
+        for head in range(heads):
+            spots = slice(head * HD, (head + 1) * HD)
+            attended = jnp.concatenate([num[a, head] / tot[a, head] for a in over], axis=0)
+            attended = attended.astype(jnp.bfloat16) * signed(osign_ref[spots])[None, :].astype(jnp.bfloat16)
+            spun = (dot(attended, plane_mat_ref[...]) * pscale_ref[...]).astype(jnp.bfloat16)
+            for at, a in enumerate(over):
+                rotated[a, :, spots] = spun[at * TILE : (at + 1) * TILE]
+        for a in over:
+            ooff[a] = 1.5 * dot(rotated[a], pm[0:local, :])
+
+    def produce(g, over):
+        left = jnp.concatenate([rotated[a] for a in over], axis=0)
+        shift = jnp.concatenate([ooff[a] for a in over], axis=0)
+        result = dot(left, oweights[g])
+        for block in range(gcols // HAD):
+            lanes = slice(block * HAD, (block + 1) * HAD)
+            spots = slice(g * gcols + block * HAD, g * gcols + (block + 1) * HAD)
+            value = (result[:, lanes] - shift) * (oscale_ref[spots] * (local * 4) ** -0.5)[None, :]
+            value = value.astype(jnp.bfloat16)
+            for at, a in enumerate(over):
+                piece = value[at * TILE : (at + 1) * TILE].reshape(TILE // unit, unit, HAD)
+                part[g, pl.ds(tile_at(a) * (TILE // unit), TILE // unit), :, lanes] = piece
+
+    first_base = tile_at(0) * (TILE // unit)
+    second_base = TILE // unit + (1 - chip) * 2
+    own_base = 3 * me
+
+    def cross_copy(g, k, chunk):
+        return head_copy(
+            summed.at[g, k], crossed.at[g, chunk % 3], x_send.at[g, k], x_recv.at[g, chunk % 3], chunk // 3
+        )
+
+    def arrival(g, k):
+        return head_copy(summed.at[g, k], crossed.at[g, k], x_send.at[g, k], x_recv.at[g, k], across)
+
+    def add_up(g, k, chunk):
+        summed[g, k] = (
+            part[g, chunk].astype(jnp.float32) + staged[g, k].astype(jnp.float32)
+        ).astype(jnp.bfloat16)
+        cross_copy(g, k, chunk).start()
+
+    first = [
+        head_copy(
+            part.at[g, pl.ds(first_base + 2 * (1 - core), 2)], staged.at[g, pl.ds(0, 2)],
+            p_send.at[g], p_recv.at[g], partner,
+        )
+        for g in range(groups)
+    ]
+    second = [
+        head_copy(
+            part.at[g, pl.ds(second_base + 1 - core, 1)], staged.at[g, pl.ds(2, 1)],
+            r_send.at[g], r_recv.at[g], partner,
+        )
+        for g in range(groups)
+    ]
+    flanks = [
+        head_copy(part.at[g, pl.ds(3 * partner, 3)], flank.at[g], q_send.at[g], q_recv.at[g], partner)
+        for g in range(groups)
+    ]
+
+    def relay_first(g):
+        first[g].wait_recv()
+        for k in range(2):
+            add_up(g, k, first_base + 2 * core + k)
+
+    def relay_second(g):
+        second[g].wait_recv()
+        add_up(g, 2, second_base + core)
+
+    near_wait(0)
+    near_attend(0, (0, 1))
+    near_wait(1)
+    near_attend(1, (0,))
+    complete((0,))
+    for g in range(groups):
+        produce(g, (0,))
+        first[g].start()
+        if g > 0:
+            relay_first(g - 1)
+    relay_first(groups - 1)
+    near_attend(1, (1, 2))
+    near_wait(2)
+    near_attend(2, (1, 2))
+    complete((1, 2))
+    for g in range(groups):
+        produce(g, (1, 2))
+        second[g].start()
+        flanks[g].start()
+        if g > 0:
+            relay_second(g - 1)
+    relay_second(groups - 1)
+
+    for g in range(groups):
+        flanks[g].wait_recv()
+        for k in range(3):
+            arrival(g, k).wait_recv()
+        for block in range(gcols // HAD):
+            lanes = slice(block * HAD, (block + 1) * HAD)
+            spots = slice(g * gcols + block * HAD, g * gcols + (block + 1) * HAD)
+            total = part[g, pl.ds(own_base, 3), :, lanes].astype(jnp.float32)
+            total = total + flank[g, :, :, lanes].astype(jnp.float32)
+            total = total + crossed[g, :, :, lanes].astype(jnp.float32)
+            spun = rotate_split(total.reshape(3 * unit, HAD), mat_ref[...])
+            out_ref[:, spots] = (spun * signed(outsign_ref[spots])[None, :]).astype(jnp.bfloat16)
+
+    for copy in crossing + relays + [beside] + first + second + flanks:
+        copy.wait_send()
+    for g in range(groups):
+        for k in range(3):
+            arrival(g, k).wait_send()
+    for slot in range(2):
+
+        @pl.when(gives[slot])
+        def _():
+            for step in range(steps):
+                for c in range(per_part):
+                    halo_copy(slot, step, c).wait_send()
+
+
+def quad_call(peers, own, in_sign, qkv_codes, qkv_scale, qkv_sign, windows, oin_sign, out_codes, out_scale, out_sign):
+    rows, width = own.shape
+    local = qkv_scale.shape[1]
+    features = out_codes.shape[1]
+    cols = 2 * HD
+    count = 3 * local // cols
+    per_part = count // 3
+    inner = qkv_codes.shape[0]
+    gcols = 1024
+    groups = features // gcols
+    steps = rows // TILE
+    heads = local // HD
+    unit = rows // 12
+    dma = pltpu.SemaphoreType.DMA
+    bf16, f32 = jnp.bfloat16, jnp.float32
+    vmem = pl.BlockSpec(memory_space=pltpu.VMEM)
+    anywhere = pl.BlockSpec(memory_space=pl.ANY)
+    smem = pl.BlockSpec(memory_space=pltpu.SMEM)
+    triple = pltpu.VMEM((groups, 3, unit, gcols), bf16)
+    return pl.pallas_call(
+        functools.partial(quad_kernel, peers),
+        name="layer",
+        out_shape=jax.ShapeDtypeStruct((rows // 4, features), bf16),
+        in_specs=[vmem] * 4 + [smem] + [vmem] * 7 + [anywhere] * 2,
+        out_specs=vmem,
+        scratch_shapes=[
+            pltpu.VMEM((2, steps, TILE, width), bf16),
+            pltpu.VMEM((2, steps, TILE, width), bf16),
+            pltpu.VMEM((count, inner, cols), jnp.int32),
+            pltpu.VMEM((2, width, cols), bf16),
+            pltpu.VMEM((count, 2, width, cols), bf16),
+            pltpu.VMEM((count, steps, TILE, cols), f32),
+            pltpu.VMEM((steps, TILE, HD), f32),
+            pltpu.VMEM((TILE, HD), f32),
+            pltpu.VMEM((width, HD), bf16),
+            pltpu.VMEM((count, 16, cols), f32),
+            pltpu.VMEM((4, 8, width), f32),
+            pltpu.VMEM((steps, per_part, 2, TILE, cols), bf16),
+            pltpu.VMEM((steps, per_part, TILE, cols), bf16),
+            pltpu.VMEM((2, steps, per_part, 2, TILE, cols), bf16),
+            pltpu.VMEM(out_codes.shape, jnp.int32),
+            pltpu.VMEM((groups, local, gcols), bf16),
+            pltpu.VMEM((steps, heads, TILE, HD), f32),
+            pltpu.VMEM((steps, heads, TILE, HD), f32),
+            pltpu.VMEM((steps, 8, rows), f32),
+            pltpu.VMEM((steps, steps, 8, 2 * TILE), f32),
+            pltpu.VMEM((steps, TILE, local), bf16),
+            pltpu.VMEM((steps, TILE, HD), f32),
+            pltpu.VMEM((groups, 12, unit, gcols), bf16),
+            triple,
+            triple,
+            triple,
+            triple,
+            dma((count,)),
+            dma,
+            dma((steps,)),
+            dma((steps,)),
+            dma((steps,)),
+            dma((steps,)),
+            dma,
+            dma,
+            dma((2, steps, per_part)),
+            dma((2, steps, per_part)),
+            dma((groups,)),
+            dma((groups,)),
+            dma((groups,)),
+            dma((groups,)),
+            dma((groups,)),
+            dma((groups,)),
+            dma((groups, 3)),
+            dma((groups, 3)),
+        ],
+        compiler_params=pltpu.CompilerParams(
+            collective_id=0, has_side_effects=True, vmem_limit_bytes=VLIMIT
+        ),
+    )(
+        own,
+        in_sign,
+        qkv_scale,
+        qkv_sign,
+        jnp.transpose(windows, (1, 0, 2)),
+        oin_sign,
+        out_scale,
+        out_sign,
+        plane_matrix(),
+        plain_matrix(),
+        plane_scale(),
+        power_matrix(),
+        jnp.transpose(qkv_codes, (1, 0, 2)),
+        out_codes,
+    )
+
+
 def on_device(
     n,
     peers,
@@ -420,6 +920,12 @@
     rows, width = own.shape
     local = qkv_scale.shape[1]
     features = out_codes.shape[1]
+    fitting = rows == 3 * TILE and local % (2 * HD) == 0 and features % 1024 == 0
+    if n == 4 and peers <= HROWS and fitting:
+        return quad_call(
+            peers, own, in_sign, qkv_codes, qkv_scale, qkv_sign, windows,
+            oin_sign, out_codes, out_scale, out_sign,
+        )[None]
     reach = (1,) if peers <= HROWS else (1, HROWS - 1, HROWS, HROWS + 1)
     distances = tuple(d for r in reach if r < peers for d in (r, -r))
     slots = len(distances)

time: 52.9 us -> 49.5 us (0.936)
  the two profiles are of different devices: /device:TPU:0 before, /device:TPU:1 now
where the time goes in v1:
time: 49.5 us; the launch traced here: 49.3 us
  Pallas kernels  47.5 us (96%)
  local copies, waits for them, and re-layouts  1.84 us (4%)
    pallas_call x1, Pallas kernels, quad_call(): pl.pallas_call(functools.partial(quad_kernel, peers), name='layer', out_s...  47.5 us
    unnamed x1, local copies, waits for them, and re-layouts  1.84 us

profile of v1, /device:TPU:1, one launch (start us, length us, event | category | flops | bytes accessed | tf_op | source)
XLA Modules:
  0.0 49.3 jit_solution(5870711809680844256)
XLA Ops:
  0.0 47.5 %layer.1 = bf16[48,5120]{1,0:T(8,128)(2,1)} custom-call(bf16[192,1280]{1,0:T(8,128)(2,1)} %bitcast.6, s32[5120]{0:T(1024)} %insigns_ref.1, f32[3,768]{1,0:T(4,128)} %qscale_ref.1, s32[3,768]{1,0:T(4,128)} %qsign_ref.1, s32[3,1,27]{2,1,0:T(1,128)} %bitcast.7, s32[768]{0:T(1024)} %osign_ref.1, f32[5120]{0:T(1024)} %oscale_ref.1, s32[5120]{0:T(1024)} %outsign_ref.1, ...), custom_call_target="tpu_custom_call" | custom-call | tf_op jit(solution)/shard_map/layer/pallas_call | solution.py:831
  47.5 1.8 %copy.16 = bf16[1,48,5120]{2,1,0:T(8,128)(2,1)} copy(bf16[1,48,5120]{2,1,0:T(8,128)(2,1)} %bitcast.5) | data formatting | bytes 983040

commit v2 on v1

--- a/solution.py
+++ b/solution.py
@@ -571,20 +571,29 @@
             device_id={"height": row + distances[slot]}, device_id_type=MESH,
         )
 
-    def project(step):
-        late = dot(late_x[0, step], pm[...]) + dot(late_x[1, step], pm[...])
-        offs[...] = 1.5 * (eoff[step] + late)
+    def shift_of(over):
+        span = slice(over[0], over[-1] + 1)
+        size = len(over) * TILE
+        late = dot(late_x[0, span].reshape(size, width), pm[...])
+        late = late + dot(late_x[1, span].reshape(size, width), pm[...])
+        offs[span] = 1.5 * (eoff[span] + late.reshape(len(over), TILE, HD))
+
+    def project(over, kinds):
+        span = slice(over[0], over[-1] + 1)
+        size = len(over) * TILE
 
         @pl.loop(0, per_part)
         def _(c):
-            for kind in range(3):
+            for kind in kinds:
                 j = kind * per_part + c
-                result = acc[j, step] + dot(late_x[0, step], late_w[j, 0])
-                result = result + dot(late_x[1, step], late_w[j, 1])
+                result = acc[j, span].reshape(size, cols)
+                result = result + dot(late_x[0, span].reshape(size, width), late_w[j, 0])
+                result = result + dot(late_x[1, span].reshape(size, width), late_w[j, 1])
+                shift = offs[span].reshape(size, HD)
                 stack, factors = [], []
                 for head in range(per_chunk):
                     lanes = slice(head * HD, (head + 1) * HD)
-                    block = (result[:, lanes] - offs[...]) * lines[j, 0:1, lanes]
+                    block = (result[:, lanes] - shift) * lines[j, 0:1, lanes]
                     high = block.astype(jnp.bfloat16)
                     stack += [high, (block - high.astype(jnp.float32)).astype(jnp.bfloat16)]
                     if kind != 1:
@@ -593,19 +602,31 @@
                 spun = dot(jnp.concatenate(stack, axis=0), mat_ref[...])
                 for head in range(per_chunk):
                     lanes = slice(head * HD, (head + 1) * HD)
-                    at = 2 * head * TILE
-                    value = (spun[at : at + TILE] + spun[at + TILE : at + 2 * TILE]) * lines[j, 8:9, lanes]
+                    at = 2 * head * size
+                    value = (spun[at : at + size] + spun[at + size : at + 2 * size]) * lines[j, 8:9, lanes]
                     if kind != 1:
                         value = value * factors[head]
-                    if kind == 2:
-                        queries[step, c, :, lanes] = value.astype(jnp.bfloat16)
-                    else:
-                        kv[step, c, kind, :, lanes] = value.astype(jnp.bfloat16)
+                    value = value.astype(jnp.bfloat16).reshape(len(over), TILE, HD)
+                    for k, a in enumerate(over):
+                        if kind == 2:
+                            queries[a, c, :, lanes] = value[k]
+                        else:
+                            kv[a, c, kind, :, lanes] = value[k]
+            if kinds == (0, 1):
+                for slot in range(2):
+
+                    @pl.when(gives[slot])
+                    def _():
+                        halo_copy(slot, over[0], c).start()
+
+        if kinds == (0, 1):
             for slot in range(2):
 
                 @pl.when(gives[slot])
                 def _():
-                    halo_copy(slot, step, c).start()
+                    for a in over[1:]:
+                        for c in range(per_part):
+                            halo_copy(slot, a, c).start()
 
     @pl.loop(0, count - 2)
     def _(j):
@@ -619,26 +640,23 @@
         prepare(j)
 
     relays[0].wait_recv()
-    project(0)
+    shift_of((0,))
+    project((0,), (0, 1))
     crossing[1].wait_recv()
     relays[1].start()
     fetch_out.wait()
 
-    @pl.loop(0, 2)
+    @pl.loop(0, groups)
     def _(c):
         spread(c)
 
     relays[1].wait_recv()
-    project(1)
     crossing[2].wait_recv()
     relays[2].start()
-
-    @pl.loop(2, groups)
-    def _(c):
-        spread(c)
-
     relays[2].wait_recv()
-    project(2)
+    shift_of((1, 2))
+    project((1, 2), (0, 1))
+    project((0, 1, 2), (2,))
 
     def attend(rows_q, keys, values, mask):
         score = lax.dot_general(
@@ -842,7 +860,7 @@
             pltpu.VMEM((count, 2, width, cols), bf16),
             pltpu.VMEM((count, steps, TILE, cols), f32),
             pltpu.VMEM((steps, TILE, HD), f32),
-            pltpu.VMEM((TILE, HD), f32),
+            pltpu.VMEM((steps, TILE, HD), f32),
             pltpu.VMEM((width, HD), bf16),
             pltpu.VMEM((count, 16, cols), f32),
             pltpu.VMEM((4, 8, width), f32),

time: 49.5 us -> 45.9 us (0.927)
  Pallas kernels: 47.5 us -> 43.9 us
    pallas_call x1, Pallas kernels: 47.5 us -> 43.9 us  [quad_call(): pl.pallas_call(functools.partial(quad_kernel, peers), name='layer', out_s...]
where the time goes in v2:
time: 45.9 us; the launch traced here: 45.7 us
  Pallas kernels  43.9 us (96%)
  local copies, waits for them, and re-layouts  1.84 us (4%)
    pallas_call x1, Pallas kernels, quad_call(): pl.pallas_call(functools.partial(quad_kernel, peers), name='layer', out_s...  43.9 us
    unnamed x1, local copies, waits for them, and re-layouts  1.84 us

profile of v2, /device:TPU:1, one launch (start us, length us, event | category | flops | bytes accessed | tf_op | source)
XLA Modules:
  0.0 45.7 jit_solution(17145759671478694123)
XLA Ops:
  0.0 43.9 %layer.1 = bf16[48,5120]{1,0:T(8,128)(2,1)} custom-call(bf16[192,1280]{1,0:T(8,128)(2,1)} %bitcast.6, s32[5120]{0:T(1024)} %insigns_ref.1, f32[3,768]{1,0:T(4,128)} %qscale_ref.1, s32[3,768]{1,0:T(4,128)} %qsign_ref.1, s32[3,1,27]{2,1,0:T(1,128)} %bitcast.7, s32[768]{0:T(1024)} %osign_ref.1, f32[5120]{0:T(1024)} %oscale_ref.1, s32[5120]{0:T(1024)} %outsign_ref.1, ...), custom_call_target="tpu_custom_call" | custom-call | tf_op jit(solution)/shard_map/layer/pallas_call | solution.py:849
  43.9 1.8 %copy.16 = bf16[1,48,5120]{2,1,0:T(8,128)(2,1)} copy(bf16[1,48,5120]{2,1,0:T(8,128)(2,1)} %bitcast.5) | data formatting | bytes 983040
